TPU v7x, 128 devices: a whole 4x4x4 slice. The times are simulated.
128 devices in a mesh: wide: 16 (over x, z), narrow: 8 (over y, core).
Axes of the slice: x: 4, y: 4, z: 4, core: 2. Of those that a mesh axis runs over, the one named last changes fastest.
Arguments:
- tensor_slab: float32 [512, 512, 2048], P(None, 'wide', 'narrow'), may hold values from -220 to 220
- start_basis: float32 [512, 64], replicated, may hold values from -6 to 6
Outputs:
- factor_basis: float32 [512, 64], replicated
- core_unfold: float32 [2048, 64, 512], P('narrow', 'wide')
All inputs are finite; a program needn't handle non-finite values.
Results may differ from a plain program's by a relative error of at most 0.0003.
Values sent between devices are 32-bit elements; how exact they have to be, the bound alone decides.
A program may use at most 64 MiB of HBM per device.

v0:
```python
import jax
import jax.numpy as jnp
from jax import lax
from jax.sharding import PartitionSpec as P

I1 = 512
ITERS = 8


def orthonormal(block, inner):
    lower_factor = jnp.linalg.cholesky(inner)
    return jax.scipy.linalg.solve_triangular(lower_factor, block.T, lower=True).T


def shards(tensor_slab, start_basis):
    highest = lax.Precision.HIGHEST
    unfold = tensor_slab.reshape(I1, -1)
    basis = start_basis
    local_gram = jnp.dot(unfold, unfold.T, precision=highest, preferred_element_type=jnp.float32)
    gram_full = lax.psum(local_gram, ("wide", "narrow"))
    for sweep_index in range(ITERS):
        block = jnp.dot(gram_full, basis, precision=highest)
        basis = orthonormal(block, jnp.dot(block.T, block, precision=highest))
    core_local = jnp.einsum("ir,ijl->lrj", basis, tensor_slab, precision=highest)
    core_unfold = lax.all_to_all(core_local, "wide", split_axis=1, concat_axis=2, tiled=True)
    return (basis, core_unfold)


def solution(mesh):
    placed = (P(None, "wide", "narrow"), P())
    return jax.shard_map(
        shards,
        mesh=mesh,
        in_specs=placed,
        out_specs=(P(), P("narrow", "wide", None)),
        check_vma=False,
    )
```

profile of v0, /device:TPU:1, one launch (start us, length us, event | category | flops | bytes accessed | tf_op | source)
XLA Modules:
  0.0 389.1 jit_solution(11629814040123961032)
XLA Ops:
  7.2 40.1 %fusion.7 = f32[512,512]{1,0:T(8,128)} fusion(f32[512,32,256]{2,1,0:T(8,128)} %param.5), kind=kOutput, calls=%fused_computation.5 | convolution fusion | flops 25769803776 | bytes 17825792 | tf_op jit(solution)/shard_map/dot_general | solution.py:19
  47.3 150.7 %all-reduce.2.cloned.1.call-done = f32[512,512]{1,0:T(8,128)} async-done(((f32[512,512]{1,0:T(8,128)}), f32[512,512]{1,0:T(8,128)}) %all-reduce.2.cloned.1.call-update) | async-done | bytes 1048592 | tf_op jit(solution)/shard_map/psum | solution.py:20
  200.7 5.8 %cholesky.134 = f32[64,64]{1,0:T(8,128)S(1)} custom-call(f32[64,64]{1,0:T(8,128)S(1)} %fusion.50), custom_call_target="Cholesky" | custom-call | tf_op jit(solution)/shard_map/jit(cholesky)/cholesky | solution.py:11
  207.9 4.9 %custom-call.12 = f32[1,64,64]{1,2,0:T(8,128)S(1)} custom-call(f32[1,64,64]{2,1,0:T(8,128)S(1)} %fusion.27), custom_call_target="InvertDiagBlocksLowerTriangular" | custom-call | tf_op jit(solution)/shard_map/jit(_solve_triangular)/triangular_solve | solution.py:12
  213.2 2.4 fusion.67
  215.9 5.8 %cholesky.145 = f32[64,64]{1,0:T(8,128)S(1)} custom-call(f32[64,64]{1,0:T(8,128)S(1)} %fusion.48), custom_call_target="Cholesky" | custom-call | tf_op jit(solution)/shard_map/jit(cholesky)/cholesky | solution.py:11
  223.1 4.9 %custom-call.13 = f32[1,64,64]{1,2,0:T(8,128)S(1)} custom-call(f32[1,64,64]{2,1,0:T(8,128)S(1)} %fusion.28), custom_call_target="InvertDiagBlocksLowerTriangular" | custom-call | tf_op jit(solution)/shard_map/jit(_solve_triangular)/triangular_solve | solution.py:12
  231.0 5.8 %cholesky.156 = f32[64,64]{1,0:T(8,128)S(1)} custom-call(f32[64,64]{1,0:T(8,128)S(1)} %fusion.46), custom_call_target="Cholesky" | custom-call | tf_op jit(solution)/shard_map/jit(cholesky)/cholesky | solution.py:11
  238.2 4.9 %custom-call.14 = f32[1,64,64]{1,2,0:T(8,128)S(1)} custom-call(f32[1,64,64]{2,1,0:T(8,128)S(1)} %fusion.29), custom_call_target="InvertDiagBlocksLowerTriangular" | custom-call | tf_op jit(solution)/shard_map/jit(_solve_triangular)/triangular_solve | solution.py:12
  243.5 2.4 fusion.71
  246.2 5.8 %cholesky.167 = f32[64,64]{1,0:T(8,128)S(1)} custom-call(f32[64,64]{1,0:T(8,128)S(1)} %fusion.44), custom_call_target="Cholesky" | custom-call | tf_op jit(solution)/shard_map/jit(cholesky)/cholesky | solution.py:11
  253.4 4.9 %custom-call.15 = f32[1,64,64]{1,2,0:T(8,128)S(1)} custom-call(f32[1,64,64]{2,1,0:T(8,128)S(1)} %fusion.30), custom_call_target="InvertDiagBlocksLowerTriangular" | custom-call | tf_op jit(solution)/shard_map/jit(_solve_triangular)/triangular_solve | solution.py:12
  258.6 2.5 fusion.73
  261.5 5.8 %cholesky.178 = f32[64,64]{1,0:T(8,128)S(1)} custom-call(f32[64,64]{1,0:T(8,128)S(1)} %fusion.42), custom_call_target="Cholesky" | custom-call | tf_op jit(solution)/shard_map/jit(cholesky)/cholesky | solution.py:11
  268.7 4.9 %custom-call.16 = f32[1,64,64]{1,2,0:T(8,128)S(1)} custom-call(f32[1,64,64]{2,1,0:T(8,128)S(1)} %fusion.31), custom_call_target="InvertDiagBlocksLowerTriangular" | custom-call | tf_op jit(solution)/shard_map/jit(_solve_triangular)/triangular_solve | solution.py:12
  273.9 2.4 fusion.75
  276.6 5.8 %cholesky.189 = f32[64,64]{1,0:T(8,128)S(1)} custom-call(f32[64,64]{1,0:T(8,128)S(1)} %fusion.40), custom_call_target="Cholesky" | custom-call | tf_op jit(solution)/shard_map/jit(cholesky)/cholesky | solution.py:11
  283.8 4.9 %custom-call.17 = f32[1,64,64]{1,2,0:T(8,128)S(1)} custom-call(f32[1,64,64]{2,1,0:T(8,128)S(1)} %fusion.32), custom_call_target="InvertDiagBlocksLowerTriangular" | custom-call | tf_op jit(solution)/shard_map/jit(_solve_triangular)/triangular_solve | solution.py:12
  291.8 5.8 %cholesky.200 = f32[64,64]{1,0:T(8,128)S(1)} custom-call(f32[64,64]{1,0:T(8,128)S(1)} %fusion.38), custom_call_target="Cholesky" | custom-call | tf_op jit(solution)/shard_map/jit(cholesky)/cholesky | solution.py:11
  299.0 4.9 %custom-call.18 = f32[1,64,64]{1,2,0:T(8,128)S(1)} custom-call(f32[1,64,64]{2,1,0:T(8,128)S(1)} %fusion.33), custom_call_target="InvertDiagBlocksLowerTriangular" | custom-call | tf_op jit(solution)/shard_map/jit(_solve_triangular)/triangular_solve | solution.py:12
  306.9 5.8 %cholesky.211 = f32[64,64]{1,0:T(8,128)S(1)} custom-call(f32[64,64]{1,0:T(8,128)S(1)} %fusion.36), custom_call_target="Cholesky" | custom-call | tf_op jit(solution)/shard_map/jit(cholesky)/cholesky | solution.py:11
  314.1 4.9 %custom-call.19 = f32[1,64,64]{1,2,0:T(8,128)S(1)} custom-call(f32[1,64,64]{2,1,0:T(8,128)S(1)} %fusion.34), custom_call_target="InvertDiagBlocksLowerTriangular" | custom-call | tf_op jit(solution)/shard_map/jit(_solve_triangular)/triangular_solve | solution.py:12
  319.4 25.8 %fusion.4 = f32[256,64,32]{0,1,2:T(8,128)S(1)} fusion(f32[512,32,256]{2,1,0:T(8,128)} %param.5, f32[64,512]{1,0:T(8,128)S(1)} %fusion.11), kind=kOutput, calls=%fused_computation.4 | convolution fusion | flops 3221225472 | bytes 19005440 | tf_op jit(solution)/shard_map/ir,ijl->lrj/dot_general | solution.py:24
  346.4 33.5 %all_to_all.18 = f32[256,64,32]{0,2,1:T(8,128)S(1)} all-to-all(f32[256,64,32]{0,2,1:T(8,128)S(1)} %copy.53), channel_id=1, replica_groups=mesh['wide'=16,'narrow'=8] {'wide'}, dimensions={1} | all-to-all | bytes 4194304 | tf_op jit(solution)/shard_map/all_to_all | solution.py:25
  (69 shorter events, 28.9 us)
Async XLA Ops:
  7.2 190.9 %copy-start = (f32[512,64]{0,1:T(8,128)S(1)}, f32[512,64]{0,1:T(8,128)}, u32[]{:S(2)}) copy-start(f32[512,64]{0,1:T(8,128)} %param.6) | copy-start | bytes 393220
  7.2 190.9 %all-reduce.2.cloned.1.call-start = ((), (), s32[]{:S(2)}) async-start(), calls=%async_computation.1 | async-start | bytes 2097152 | tf_op jit(solution)/shard_map/psum | solution.py:20
  319.4 62.7 %copy-start.1 = (f32[64,512]{1,0:T(8,128)}, f32[64,512]{1,0:T(8,128)S(1)}, u32[]{:S(2)}) copy-start(f32[64,512]{1,0:T(8,128)S(1)} %fusion.11) | copy-start | bytes 393220
Sparse Core Ops, SparseCore 0:
  47.4 150.5 all-reduce.1
where the time goes:
time: 393 us; the launch traced here: 389 us
  waiting for transfers between devices  151 us (38%)
  other arithmetic  96.6 us (25%)
  matrix products  89.7 us (23%)
  blocking collectives  33.5 us (9%)
  between operations  14.6 us (4%)
  local copies, waits for them, and re-layouts  3.93 us (1%)
    psum x1, waiting for transfers between devices, shards(): gram_full = lax.psum(local_gram, ('wide', 'narrow'))  151 us
    another operation x24, other arithmetic, orthonormal(): lower_factor = jnp.linalg.cholesky(inner)  52.2 us
    another operation x16, other arithmetic, orthonormal(): jax.scipy.linalg.solve_triangular(lower_factor, block.T, lower=True)  44.4 us
    dot_general x1, matrix products, shards(): jnp.dot(unfold, unfold.T, precision=highest, preferred_element_type=jnp.f...  40.1 us
    all_to_all x1, blocking collectives, shards(): lax.all_to_all(core_local, 'wide', split_axis=1, concat_axis=2, tiled=True)  33.5 us
    dot_general x1, matrix products, shards(): jnp.einsum('ir,ijl->lrj', basis, tensor_slab, precision=highest)  25.8 us
    dot_general x8, matrix products, shards(): block = jnp.dot(gram_full, basis, precision=highest)  19 us
  transfers between devices with their start and end apart: 1, of which 1 were waited for; matrix products, arithmetic and copies ran while one was open for 0% of the time, Pallas kernels for 0%

commit v1 on v0

--- a/solution.py
+++ b/solution.py
@@ -5,6 +5,13 @@
 
 I1 = 512
 ITERS = 8
+
+
+def stacked_exchange(block, mesh_axis, split, join):
+    size = lax.axis_size(mesh_axis)
+    blocks = jnp.stack(jnp.split(block, size, axis=split), axis=0)
+    blocks = lax.all_to_all(blocks, mesh_axis, split_axis=0, concat_axis=0)
+    return jnp.concatenate(blocks, axis=join)
 
 
 def orthonormal(block, inner):
@@ -22,7 +29,7 @@
         block = jnp.dot(gram_full, basis, precision=highest)
         basis = orthonormal(block, jnp.dot(block.T, block, precision=highest))
     core_local = jnp.einsum("ir,ijl->lrj", basis, tensor_slab, precision=highest)
-    core_unfold = lax.all_to_all(core_local, "wide", split_axis=1, concat_axis=2, tiled=True)
+    core_unfold = stacked_exchange(core_local, "wide", 1, 2)
     return (basis, core_unfold)
 
 

time: 393 us -> 384 us (0.977)
  matrix products: 89.7 us -> 81.3 us
    dot_general x8, matrix products: 19 us -> 10.6 us  [shards(): block = jnp.dot(gram_full, basis, precision=highest)]
where the time goes in v1:
time: 384 us; the launch traced here: 381 us
  waiting for transfers between devices  151 us (39%)
  other arithmetic  96.6 us (25%)
  matrix products  81.3 us (21%)
  blocking collectives  33.5 us (9%)
  between operations  14.7 us (4%)
    psum x1, waiting for transfers between devices, shards(): gram_full = lax.psum(local_gram, ('wide', 'narrow'))  151 us
    another operation x24, other arithmetic, orthonormal(): lower_factor = jnp.linalg.cholesky(inner)  52.2 us
    another operation x16, other arithmetic, orthonormal(): jax.scipy.linalg.solve_triangular(lower_factor, block.T, lower=True)  44.4 us
    dot_general x1, matrix products, shards(): jnp.dot(unfold, unfold.T, precision=highest, preferred_element_type=jnp.f...  40.1 us
    all_to_all x1, blocking collectives, stacked_exchange(): blocks = lax.all_to_all(blocks, mesh_axis, split_axis=0, concat_axis=0)  33.5 us
    dot_general x1, matrix products, shards(): jnp.einsum('ir,ijl->lrj', basis, tensor_slab, precision=highest)  25.8 us
    dot_general x8, matrix products, shards(): block = jnp.dot(gram_full, basis, precision=highest)  10.6 us
  transfers between devices with their start and end apart: 1, of which 1 were waited for; matrix products, arithmetic and copies ran while one was open for 0% of the time, Pallas kernels for 0%

profile of v1, /device:TPU:1, one launch (start us, length us, event | category | flops | bytes accessed | tf_op | source)
XLA Modules:
  0.0 380.5 jit_solution(2024902462358372228)
XLA Ops:
  7.2 40.1 %fusion.7 = f32[512,512]{1,0:T(8,128)} fusion(f32[512,32,256]{2,1,0:T(8,128)} %param.5), kind=kOutput, calls=%fused_computation.5 | convolution fusion | flops 25769803776 | bytes 17825792 | tf_op jit(solution)/shard_map/dot_general | solution.py:26
  47.3 150.7 %all-reduce.2.cloned.1.call-done = f32[512,512]{1,0:T(8,128)} async-done(((f32[512,512]{1,0:T(8,128)}), f32[512,512]{1,0:T(8,128)}) %all-reduce.2.cloned.1.call-update) | async-done | bytes 1048592 | tf_op jit(solution)/shard_map/psum | solution.py:27
  198.0 2.4 fusion.81
  200.8 5.8 %cholesky.134 = f32[64,64]{1,0:T(8,128)S(1)} custom-call(f32[64,64]{1,0:T(8,128)S(1)} %fusion.66), custom_call_target="Cholesky" | custom-call | tf_op jit(solution)/shard_map/jit(cholesky)/cholesky | solution.py:18
  208.0 4.9 %custom-call.12 = f32[1,64,64]{1,2,0:T(8,128)S(1)} custom-call(f32[1,64,64]{2,1,0:T(8,128)S(1)} %fusion.43), custom_call_target="InvertDiagBlocksLowerTriangular" | custom-call | tf_op jit(solution)/shard_map/jit(_solve_triangular)/triangular_solve | solution.py:19
  214.8 5.8 %cholesky.145 = f32[64,64]{1,0:T(8,128)S(1)} custom-call(f32[64,64]{1,0:T(8,128)S(1)} %fusion.64), custom_call_target="Cholesky" | custom-call | tf_op jit(solution)/shard_map/jit(cholesky)/cholesky | solution.py:18
  222.0 4.9 %custom-call.13 = f32[1,64,64]{1,2,0:T(8,128)S(1)} custom-call(f32[1,64,64]{2,1,0:T(8,128)S(1)} %fusion.44), custom_call_target="InvertDiagBlocksLowerTriangular" | custom-call | tf_op jit(solution)/shard_map/jit(_solve_triangular)/triangular_solve | solution.py:19
  227.2 1.1 fusion.85
  228.7 5.8 %cholesky.156 = f32[64,64]{1,0:T(8,128)S(1)} custom-call(f32[64,64]{1,0:T(8,128)S(1)} %fusion.62), custom_call_target="Cholesky" | custom-call | tf_op jit(solution)/shard_map/jit(cholesky)/cholesky | solution.py:18
  235.9 4.9 %custom-call.14 = f32[1,64,64]{1,2,0:T(8,128)S(1)} custom-call(f32[1,64,64]{2,1,0:T(8,128)S(1)} %fusion.45), custom_call_target="InvertDiagBlocksLowerTriangular" | custom-call | tf_op jit(solution)/shard_map/jit(_solve_triangular)/triangular_solve | solution.py:19
  242.6 5.8 %cholesky.167 = f32[64,64]{1,0:T(8,128)S(1)} custom-call(f32[64,64]{1,0:T(8,128)S(1)} %fusion.60), custom_call_target="Cholesky" | custom-call | tf_op jit(solution)/shard_map/jit(cholesky)/cholesky | solution.py:18
  249.8 4.9 %custom-call.15 = f32[1,64,64]{1,2,0:T(8,128)S(1)} custom-call(f32[1,64,64]{2,1,0:T(8,128)S(1)} %fusion.46), custom_call_target="InvertDiagBlocksLowerTriangular" | custom-call | tf_op jit(solution)/shard_map/jit(_solve_triangular)/triangular_solve | solution.py:19
  255.1 1.3 fusion.89
  256.7 5.8 %cholesky.178 = f32[64,64]{1,0:T(8,128)S(1)} custom-call(f32[64,64]{1,0:T(8,128)S(1)} %fusion.58), custom_call_target="Cholesky" | custom-call | tf_op jit(solution)/shard_map/jit(cholesky)/cholesky | solution.py:18
  263.9 4.9 %custom-call.16 = f32[1,64,64]{1,2,0:T(8,128)S(1)} custom-call(f32[1,64,64]{2,1,0:T(8,128)S(1)} %fusion.47), custom_call_target="InvertDiagBlocksLowerTriangular" | custom-call | tf_op jit(solution)/shard_map/jit(_solve_triangular)/triangular_solve | solution.py:19
  270.7 5.8 %cholesky.189 = f32[64,64]{1,0:T(8,128)S(1)} custom-call(f32[64,64]{1,0:T(8,128)S(1)} %fusion.56), custom_call_target="Cholesky" | custom-call | tf_op jit(solution)/shard_map/jit(cholesky)/cholesky | solution.py:18
  277.8 4.9 %custom-call.17 = f32[1,64,64]{1,2,0:T(8,128)S(1)} custom-call(f32[1,64,64]{2,1,0:T(8,128)S(1)} %fusion.48), custom_call_target="InvertDiagBlocksLowerTriangular" | custom-call | tf_op jit(solution)/shard_map/jit(_solve_triangular)/triangular_solve | solution.py:19
  284.6 5.8 %cholesky.200 = f32[64,64]{1,0:T(8,128)S(1)} custom-call(f32[64,64]{1,0:T(8,128)S(1)} %fusion.54), custom_call_target="Cholesky" | custom-call | tf_op jit(solution)/shard_map/jit(cholesky)/cholesky | solution.py:18
  291.8 4.9 %custom-call.18 = f32[1,64,64]{1,2,0:T(8,128)S(1)} custom-call(f32[1,64,64]{2,1,0:T(8,128)S(1)} %fusion.49), custom_call_target="InvertDiagBlocksLowerTriangular" | custom-call | tf_op jit(solution)/shard_map/jit(_solve_triangular)/triangular_solve | solution.py:19
  298.5 5.8 %cholesky.211 = f32[64,64]{1,0:T(8,128)S(1)} custom-call(f32[64,64]{1,0:T(8,128)S(1)} %fusion.52), custom_call_target="Cholesky" | custom-call | tf_op jit(solution)/shard_map/jit(cholesky)/cholesky | solution.py:18
  305.7 4.9 %custom-call.19 = f32[1,64,64]{1,2,0:T(8,128)S(1)} custom-call(f32[1,64,64]{2,1,0:T(8,128)S(1)} %fusion.50), custom_call_target="InvertDiagBlocksLowerTriangular" | custom-call | tf_op jit(solution)/shard_map/jit(_solve_triangular)/triangular_solve | solution.py:19
  311.0 25.8 %fusion.4 = f32[256,64,32]{0,1,2:T(8,128)S(1)} fusion(f32[512,32,256]{2,1,0:T(8,128)} %param.5, f32[64,512]{1,0:T(8,128)S(1)} %fusion.27), kind=kOutput, calls=%fused_computation.4 | convolution fusion | flops 3221225472 | bytes 19005440 | tf_op jit(solution)/shard_map/ir,ijl->lrj/dot_general | solution.py:31
  337.5 33.5 %all_to_all.5 = f32[16,256,4,32]{1,2,3,0:T(4,128)S(1)} all-to-all(f32[16,256,4,32]{1,2,3,0:T(4,128)S(1)} %fusion.10), channel_id=1, replica_groups=mesh['wide'=16,'narrow'=8] {'wide'}, dimensions={0} | all-to-all | bytes 4194304 | tf_op jit(solution)/shard_map/all_to_all | solution.py:13
  371.0 2.5 copy.15
  (85 shorter events, 22.4 us)
Async XLA Ops:
  7.2 190.9 %copy-start = (f32[512,64]{0,1:T(8,128)S(1)}, f32[512,64]{0,1:T(8,128)}, u32[]{:S(2)}) copy-start(f32[512,64]{0,1:T(8,128)} %param.6) | copy-start | bytes 393220
  7.2 190.9 %all-reduce.2.cloned.1.call-start = ((), (), s32[]{:S(2)}) async-start(), calls=%async_computation.1 | async-start | bytes 2097152 | tf_op jit(solution)/shard_map/psum | solution.py:27
  198.0 15.2 %copy-start.1 = (f32[512,512]{1,0:T(8,128)S(1)}, f32[512,512]{1,0:T(8,128)}, u32[]{:S(2)}) copy-start(f32[512,512]{1,0:T(8,128)} %all-reduce.2.cloned.1.call-done) | copy-start | bytes 3145732
  310.9 25.8 %copy-start.2 = (f32[64,512]{1,0:T(8,128)}, f32[64,512]{1,0:T(8,128)S(1)}, u32[]{:S(2)}) copy-start(f32[64,512]{1,0:T(8,128)S(1)} %fusion.27) | copy-start | bytes 393220
Sparse Core Ops, SparseCore 0:
  47.4 150.5 all-reduce.1

commit v2 on v0

--- a/solution.py
+++ b/solution.py
@@ -17,7 +17,8 @@
     unfold = tensor_slab.reshape(I1, -1)
     basis = start_basis
     local_gram = jnp.dot(unfold, unfold.T, precision=highest, preferred_element_type=jnp.float32)
-    gram_full = lax.psum(local_gram, ("wide", "narrow"))
+    note_the_flows = lambda inp: lax.psum(lax.psum(inp, "narrow"), "wide")
+    gram_full = note_the_flows(local_gram)
     for sweep_index in range(ITERS):
         block = jnp.dot(gram_full, basis, precision=highest)
         basis = orthonormal(block, jnp.dot(block.T, block, precision=highest))

time: 393 us -> 395 us (level)
    psum x1 -> x2, waiting for transfers between devices: 151 us -> 154 us  [shards(): note_the_flows = lambda inp: lax.psum(lax.psum(inp, 'narrow'), 'wide')]
  transfers between devices with their start and end apart: 1 -> 2, of which waited for: 1 -> 2; matrix products, arithmetic and copies ran while one was open for 0% -> 0% of each run, Pallas kernels for 0% -> 0%
where the time goes in v2:
time: 395 us; the launch traced here: 388 us
  waiting for transfers between devices  154 us (39%)
  other arithmetic  96.6 us (24%)
  matrix products  89.3 us (23%)
  blocking collectives  29.7 us (8%)
  between operations  14.6 us (4%)
    psum x2, waiting for transfers between devices, shards(): note_the_flows = lambda inp: lax.psum(lax.psum(inp, 'narrow'), 'wide')  154 us
    another operation x24, other arithmetic, orthonormal(): lower_factor = jnp.linalg.cholesky(inner)  52.2 us
    another operation x16, other arithmetic, orthonormal(): jax.scipy.linalg.solve_triangular(lower_factor, block.T, lower=True)  44.4 us
    dot_general x1, matrix products, shards(): jnp.dot(unfold, unfold.T, precision=highest, preferred_element_type=jnp.f...  39.6 us
    all_to_all x1, blocking collectives, shards(): lax.all_to_all(core_local, 'wide', split_axis=1, concat_axis=2, tiled=True)  29.7 us
    dot_general x1, matrix products, shards(): jnp.einsum('ir,ijl->lrj', basis, tensor_slab, precision=highest)  25.8 us
    dot_general x8, matrix products, shards(): block = jnp.dot(gram_full, basis, precision=highest)  19 us
  transfers between devices with their start and end apart: 2, of which 2 were waited for; matrix products, arithmetic and copies ran while one was open for 0% of the time, Pallas kernels for 0%

profile of v2, /device:TPU:1, one launch (start us, length us, event | category | flops | bytes accessed | tf_op | source)
XLA Modules:
  0.0 388.3 jit_solution(10088945790546932113)
XLA Ops:
  7.2 39.6 %fusion.7 = f32[512,512]{1,0:T(8,128)} fusion(f32[512,32,256]{2,1,0:T(8,128)} %param.5), kind=kOutput, calls=%fused_computation.5 | convolution fusion | flops 25769803776 | bytes 17825792 | tf_op jit(solution)/shard_map/dot_general | solution.py:19
  47.4 63.3 %all-reduce.3.cloned.1.call-done = f32[512,512]{1,0:T(8,128)} async-done(((f32[512,512]{1,0:T(8,128)}), f32[512,512]{1,0:T(8,128)}) %all-reduce.3.cloned.1.call-update) | async-done | bytes 1048592 | tf_op jit(solution)/shard_map/psum | solution.py:20
  110.7 90.3 %all-reduce.5.cloned.1.call-done = f32[512,512]{1,0:T(8,128)} async-done(((f32[512,512]{1,0:T(8,128)}), f32[512,512]{1,0:T(8,128)}) %all-reduce.5.cloned.1.call-update) | async-done | bytes 1048592 | tf_op jit(solution)/shard_map/psum | solution.py:20
  203.7 5.8 %cholesky.134 = f32[64,64]{1,0:T(8,128)S(1)} custom-call(f32[64,64]{1,0:T(8,128)S(1)} %fusion.50), custom_call_target="Cholesky" | custom-call | tf_op jit(solution)/shard_map/jit(cholesky)/cholesky | solution.py:11
  210.9 4.9 %custom-call.12 = f32[1,64,64]{1,2,0:T(8,128)S(1)} custom-call(f32[1,64,64]{2,1,0:T(8,128)S(1)} %fusion.27), custom_call_target="InvertDiagBlocksLowerTriangular" | custom-call | tf_op jit(solution)/shard_map/jit(_solve_triangular)/triangular_solve | solution.py:12
  216.1 2.4 fusion.67
  218.8 5.8 %cholesky.145 = f32[64,64]{1,0:T(8,128)S(1)} custom-call(f32[64,64]{1,0:T(8,128)S(1)} %fusion.48), custom_call_target="Cholesky" | custom-call | tf_op jit(solution)/shard_map/jit(cholesky)/cholesky | solution.py:11
  226.0 4.9 %custom-call.13 = f32[1,64,64]{1,2,0:T(8,128)S(1)} custom-call(f32[1,64,64]{2,1,0:T(8,128)S(1)} %fusion.28), custom_call_target="InvertDiagBlocksLowerTriangular" | custom-call | tf_op jit(solution)/shard_map/jit(_solve_triangular)/triangular_solve | solution.py:12
  231.3 2.4 fusion.69
  234.0 5.8 %cholesky.156 = f32[64,64]{1,0:T(8,128)S(1)} custom-call(f32[64,64]{1,0:T(8,128)S(1)} %fusion.46), custom_call_target="Cholesky" | custom-call | tf_op jit(solution)/shard_map/jit(cholesky)/cholesky | solution.py:11
  241.2 4.9 %custom-call.14 = f32[1,64,64]{1,2,0:T(8,128)S(1)} custom-call(f32[1,64,64]{2,1,0:T(8,128)S(1)} %fusion.29), custom_call_target="InvertDiagBlocksLowerTriangular" | custom-call | tf_op jit(solution)/shard_map/jit(_solve_triangular)/triangular_solve | solution.py:12
  249.1 5.8 %cholesky.167 = f32[64,64]{1,0:T(8,128)S(1)} custom-call(f32[64,64]{1,0:T(8,128)S(1)} %fusion.44), custom_call_target="Cholesky" | custom-call | tf_op jit(solution)/shard_map/jit(cholesky)/cholesky | solution.py:11
  256.3 4.9 %custom-call.15 = f32[1,64,64]{1,2,0:T(8,128)S(1)} custom-call(f32[1,64,64]{2,1,0:T(8,128)S(1)} %fusion.30), custom_call_target="InvertDiagBlocksLowerTriangular" | custom-call | tf_op jit(solution)/shard_map/jit(_solve_triangular)/triangular_solve | solution.py:12
  261.6 2.5 fusion.73
  264.5 5.8 %cholesky.178 = f32[64,64]{1,0:T(8,128)S(1)} custom-call(f32[64,64]{1,0:T(8,128)S(1)} %fusion.42), custom_call_target="Cholesky" | custom-call | tf_op jit(solution)/shard_map/jit(cholesky)/cholesky | solution.py:11
  271.6 4.9 %custom-call.16 = f32[1,64,64]{1,2,0:T(8,128)S(1)} custom-call(f32[1,64,64]{2,1,0:T(8,128)S(1)} %fusion.31), custom_call_target="InvertDiagBlocksLowerTriangular" | custom-call | tf_op jit(solution)/shard_map/jit(_solve_triangular)/triangular_solve | solution.py:12
  279.6 5.8 %cholesky.189 = f32[64,64]{1,0:T(8,128)S(1)} custom-call(f32[64,64]{1,0:T(8,128)S(1)} %fusion.40), custom_call_target="Cholesky" | custom-call | tf_op jit(solution)/shard_map/jit(cholesky)/cholesky | solution.py:11
  286.8 4.9 %custom-call.17 = f32[1,64,64]{1,2,0:T(8,128)S(1)} custom-call(f32[1,64,64]{2,1,0:T(8,128)S(1)} %fusion.32), custom_call_target="InvertDiagBlocksLowerTriangular" | custom-call | tf_op jit(solution)/shard_map/jit(_solve_triangular)/triangular_solve | solution.py:12
  294.7 5.8 %cholesky.200 = f32[64,64]{1,0:T(8,128)S(1)} custom-call(f32[64,64]{1,0:T(8,128)S(1)} %fusion.38), custom_call_target="Cholesky" | custom-call | tf_op jit(solution)/shard_map/jit(cholesky)/cholesky | solution.py:11
  301.9 4.9 %custom-call.18 = f32[1,64,64]{1,2,0:T(8,128)S(1)} custom-call(f32[1,64,64]{2,1,0:T(8,128)S(1)} %fusion.33), custom_call_target="InvertDiagBlocksLowerTriangular" | custom-call | tf_op jit(solution)/shard_map/jit(_solve_triangular)/triangular_solve | solution.py:12
  309.9 5.8 %cholesky.211 = f32[64,64]{1,0:T(8,128)S(1)} custom-call(f32[64,64]{1,0:T(8,128)S(1)} %fusion.36), custom_call_target="Cholesky" | custom-call | tf_op jit(solution)/shard_map/jit(cholesky)/cholesky | solution.py:11
  317.1 4.9 %custom-call.19 = f32[1,64,64]{1,2,0:T(8,128)S(1)} custom-call(f32[1,64,64]{2,1,0:T(8,128)S(1)} %fusion.34), custom_call_target="InvertDiagBlocksLowerTriangular" | custom-call | tf_op jit(solution)/shard_map/jit(_solve_triangular)/triangular_solve | solution.py:12
  322.3 25.8 %fusion.4 = f32[256,64,32]{0,1,2:T(8,128)S(1)} fusion(f32[512,32,256]{2,1,0:T(8,128)} %param.5, f32[64,512]{1,0:T(8,128)S(1)} %fusion.11), kind=kOutput, calls=%fused_computation.4 | convolution fusion | flops 3221225472 | bytes 19005440 | tf_op jit(solution)/shard_map/ir,ijl->lrj/dot_general | solution.py:25
  349.4 29.7 %all_to_all.18 = f32[256,64,32]{0,2,1:T(8,128)S(1)} all-to-all(f32[256,64,32]{0,2,1:T(8,128)S(1)} %copy.53), channel_id=1, replica_groups=mesh['wide'=16,'narrow'=8] {'wide'}, dimensions={1} | all-to-all | bytes 4194304 | tf_op jit(solution)/shard_map/all_to_all | solution.py:26
  (72 shorter events, 31.8 us)
Async XLA Ops:
  7.2 193.8 %copy-start = (f32[512,64]{0,1:T(8,128)S(1)}, f32[512,64]{0,1:T(8,128)}, u32[]{:S(2)}) copy-start(f32[512,64]{0,1:T(8,128)} %param.6) | copy-start | bytes 393220
  7.2 103.5 %all-reduce.3.cloned.1.call-start = ((), (), s32[]{:S(2)}) async-start(), calls=%async_computation.1 | async-start | bytes 2097152 | tf_op jit(solution)/shard_map/psum | solution.py:20
  46.9 154.1 %all-reduce.5.cloned.1.call-start = ((), (), s32[]{:S(2)}) async-start(), calls=%async_computation.2 | async-start | bytes 2097152 | tf_op jit(solution)/shard_map/psum | solution.py:20
  322.3 58.9 %copy-start.1 = (f32[64,512]{1,0:T(8,128)}, f32[64,512]{1,0:T(8,128)S(1)}, u32[]{:S(2)}) copy-start(f32[64,512]{1,0:T(8,128)S(1)} %fusion.11) | copy-start | bytes 393220
Sparse Core Ops, SparseCore 0:
  47.0 63.6 all-reduce.2
  113.9 86.9 all-reduce.4
